TPU v7x, 32 devices: a whole 2x2x4 slice. The times are simulated.
32 devices in a mesh: dp: 2 (over core), seqo: 4 (over y, x), seqi: 4 (over z).
Axes of the slice: x: 2, y: 2, z: 4, core: 2. Of those that a mesh axis runs over, the one named last changes fastest.
Arguments:
- loaded: bfloat16 [4096, 1024], P(('dp', 'seqo', 'seqi')), parts along dimension 0, may hold values from -6 to 6
- packing: int32 [8, 4, 4, 2], P(('dp', 'seqo')), parts along dimension 0, may hold values from 0 to 128, as said below
- pattern: int32 [32, 64, 64], P(('dp', 'seqo', 'seqi')), parts along dimension 0, may hold values from 0 to 1, as said below
- w_query: bfloat16 [1024, 1024], replicated, may hold values from -0.1875 to 0.1875
- w_key: bfloat16 [1024, 1024], replicated, may hold values from -0.1875 to 0.1875
- w_value: bfloat16 [1024, 1024], replicated, may hold values from -0.1875 to 0.1875
- norm_gain: float32 [1024], replicated, may hold values from 0.25 to 1.75
- w_out: bfloat16 [1024, 1024], replicated, may hold values from -0.1875 to 0.1875
Outputs:
- mixed: float32 [4096, 1024], P(('dp', 'seqo', 'seqi')), parts along dimension 0
There are 2 independent parts, one for each index of `dp`. A program takes and returns all parts, laid end to end along the dimension named above; an argument that names none is the same for every part. Nothing has to cross between parts.
Inputs may be any that keep to these rules, and one draw needn't show every extreme that they name: `packing`: for each group and source s the counts over d sum to 128 and the offsets are their running sums in the order of d; for each destination d the counts over s sum to 128; a count is at most 64, and some count of every group equals 64. pattern[c, i, j] is 1 where j == i and 0 where j > i.
All inputs are finite; a program needn't handle non-finite values.
Results may differ from a plain program's by a relative error of at most 0.0053.
Values may be sent and summed in bfloat16 or wider, within the bound.
No kernel may reach another device: no remote copies, remote signals or barrier semaphores. Data moves between devices by JAX's collectives and lax.ppermute only.
A program may use at most 128 MiB of HBM per device.

v0:
```python
import jax
import jax.numpy as jnp
from jax import lax
from jax.sharding import PartitionSpec as P

H = 16
NB = 64
EPSILON = 1e-06


def prefix_2(value, axis, join, neutral):
    count, mine = (lax.axis_size(axis), lax.axis_index(axis))
    pieces = lax.all_gather(value, axis)
    so_far = jnp.full_like(value, 0) + jnp.asarray(neutral, value.dtype)

    def turn(position, so_far):
        longer = join(so_far, pieces[position])
        return jnp.where(position < mine, longer, so_far)

    return lax.fori_loop(0, count - 1, turn, so_far)


def add_states(earlier, later):
    return earlier + later


def project_columns(rows, w_query, w_key, w_value):
    return tuple(
        (
            jnp.einsum("td,de->et", rows, weight, preferred_element_type=jnp.float32).astype(
                jnp.bfloat16
            )
            for weight in (w_query, w_key, w_value)
        )
    )


def body(loaded, packing, pattern, w_query, w_key, w_value, norm_gain, w_out):
    sources = lax.axis_size("seqi")
    rows_dev = loaded.shape[0]
    feature_width = loaded.shape[1]
    capacity = 2 * rows_dev // sources
    my_index = lax.axis_index("seqi")
    source_ids = jnp.arange(sources, dtype=jnp.int32)
    select = (source_ids == my_index).astype(jnp.int32)
    table = packing[0]
    outgoing = jnp.sum(table * select[:, None, None], axis=0)
    slot_ids = jnp.arange(capacity, dtype=jnp.int32)
    valid = slot_ids[None, :] < outgoing[:, 1:2]
    slot_rows = jnp.where(valid, outgoing[:, 0:1] + slot_ids[None, :], 0)
    slots = jnp.take(loaded, slot_rows.reshape(-1), axis=0).reshape(
        sources, capacity, feature_width
    )
    slots = jnp.where(valid[:, :, None], slots, jnp.zeros((), jnp.bfloat16))
    incoming = jnp.sum(table[:, :, 1] * select[None, :], axis=1)
    ends = jnp.cumsum(incoming)
    starts = ends - incoming
    row_ids = jnp.arange(rows_dev, dtype=jnp.int32)
    source_of = jnp.sum((row_ids[:, None] >= ends[None, :]).astype(jnp.int32), axis=1)
    picked = (source_of[:, None] == source_ids[None, :]).astype(jnp.int32)
    first_row = jnp.sum(picked * starts[None, :], axis=1)
    unpack = source_of * capacity + row_ids - first_row
    arrived = lax.all_to_all(slots, "seqi", split_axis=0, concat_axis=0, tiled=True)
    tokens = jnp.take(arrived.reshape(sources * capacity, feature_width), unpack, axis=0)
    query_cols, key_cols, value_cols = project_columns(tokens, w_query, w_key, w_value)
    head_size = feature_width // H
    query_heads = query_cols.reshape(H, head_size, rows_dev)
    key_heads = key_cols.reshape(H, head_size, rows_dev)
    value_heads = value_cols.reshape(H, head_size, rows_dev)
    state = jnp.einsum("hdt,het->hde", key_heads, value_heads, preferred_element_type=jnp.float32)
    zero_state = jnp.zeros_like(state)
    inner = prefix_2(state, "seqi", add_states, zero_state)
    group_sum = lax.psum(state, "seqi")
    outer = prefix_2(group_sum, "seqo", add_states, zero_state)
    prefix = outer + inner
    scores = jnp.einsum("hdt,hds->hts", query_heads, key_heads, preferred_element_type=jnp.float32)
    frames = jnp.arange(rows_dev, dtype=jnp.int32) // (rows_dev // NB)
    allowed = pattern[0][frames][:, frames] > 0
    masked = jnp.where(allowed[None], scores, jnp.zeros((), jnp.float32)).astype(jnp.bfloat16)
    local = jnp.einsum("hts,hes->het", masked, value_heads, preferred_element_type=jnp.float32)
    carried = jnp.einsum(
        "hdt,hde->het", query_heads.astype(jnp.float32), prefix, precision=lax.Precision.HIGHEST
    )
    attended = local + carried
    factor = lax.rsqrt(jnp.mean(attended * attended, axis=1, keepdims=True) + EPSILON)
    gain = norm_gain.reshape(H, head_size, 1)
    normed = (attended * factor * gain).astype(jnp.bfloat16).reshape(feature_width, rows_dev)
    return jnp.einsum("dt,de->te", normed, w_out, preferred_element_type=jnp.float32)


def solution(mesh):
    return jax.shard_map(
        body,
        mesh=mesh,
        in_specs=(
            P(("dp", "seqo", "seqi"), None),
            P(("dp", "seqo"), None, None, None),
            P(("dp", "seqo", "seqi"), None, None),
            P(),
            P(),
            P(),
            P(),
            P(),
        ),
        out_specs=P(("dp", "seqo", "seqi"), None),
        check_vma=False,
    )
```

profile of v0, /device:TPU:0, one launch (start us, length us, event | category | flops | bytes accessed | tf_op | source)
XLA Modules:
  0.0 176.0 jit_solution(17563134460759956328)
XLA Ops:
  6.5 0.9 multiply_reduce_fusion.1
  7.5 0.1 iota_compare_fusion
  7.5 0.1 add_select_fusion.2
  7.6 0.1 select_n.137
  7.7 2.5 %gather_fusion = bf16[256,1024]{1,0:T(8,128)(2,1)S(1)} fusion(bf16[128,1024]{1,0:T(8,128)(2,1)} %param.12, s32[1024]{0:T(1024)S(1)} %pad_clamp_fusion.2), kind=kCustom, calls=%fused_computation | custom fusion | bytes 1049600 | tf_op jit(solution)/shard_map/jit(_take)/gather | solution.py:51
  10.3 0.0 copy-start.4
  10.3 0.9 select_select_fusion
  11.2 6.3 %all-to-all-start = ((bf16[4,64,1024]{2,1,0:T(8,128)(2,1)}), bf16[4,64,1024]{2,1,0:T(8,128)(2,1)S(1)}, u32[]{:S(2)}, u32[]{:S(2)}) async-start(bf16[4,64,1024]{2,1,0:T(8,128)(2,1)} %select_select_fusion), calls=%async_computation | async-start | bytes 1048576 | tf_op jit(solution)/shard_map/all_to_all | solution.py:63
  17.6 0.1 fusion.11
  17.7 0.2 reduce-window.7
  17.9 0.1 convert_reduce_fusion
  18.0 0.1 select_reduce_fusion
  18.1 14.0 %all-to-all-done = bf16[4,64,1024]{2,1,0:T(8,128)(2,1)S(1)} async-done(((bf16[4,64,1024]{2,1,0:T(8,128)(2,1)}), bf16[4,64,1024]{2,1,0:T(8,128)(2,1)S(1)}, u32[]{:S(2)}, u32[]{:S(2)}) %all-to-all-start) | async-done | bytes 524320 | tf_op jit(solution)/shard_map/all_to_all | solution.py:63
  32.1 0.9 gather_fusion.1
  32.9 0.5 fusion.3
  33.4 0.2 copy.32
  33.6 2.2 %fusion.5 = bf16[1024,128]{0,1:T(8,128)(2,1)S(1)} fusion(bf16[1024,1024]{1,0:T(8,128)(2,1)} %param.16, bf16[128,1024]{1,0:T(8,128)(2,1)S(1)} %gather_fusion.1, pred[128]{0:T(512)(128)(4,1)S(1)} %compare_and_fusion.1), kind=kOutput, calls=%fused_computation.15 | convolution fusion | flops 268697600 | bytes 2621568 | tf_op jit(solution)/shard_map/td,de->et/dot_general | solution.py:30
  35.8 0.0 copy-start.1
  35.8 0.2 copy.36
  36.0 0.0 copy-start.3
  36.0 0.0 copy-start.5
  36.0 1.1 fusion.15
  37.1 0.0 all-gather.6.cloned.1.call-update
  37.1 44.9 %all-gather.6.cloned.1.call-done = f32[64,64,64]{2,1,0:T(8,128)} async-done(((f32[16,64,64]{2,1,0:T(8,128)}), f32[64,64,64]{2,1,0:T(8,128)}) %all-gather.6.cloned.1.call-update) | async-done | bytes 1048592 | tf_op jit(solution)/shard_map/all_gather | solution.py:13
  82.0 0.7 all-reduce.2.cloned.1.call-update
  82.8 0.0 all-gather.4.cloned.1.call-start
  82.8 39.7 %all-reduce.2.cloned.1.call-done = f32[1,16,64,64]{3,2,1,0:T(8,128)} async-done(((f32[1,16,64,64]{3,2,1,0:T(8,128)}), f32[1,16,64,64]{3,2,1,0:T(8,128)}) %all-reduce.2.cloned.1.call-update) | async-done | bytes 262160 | tf_op jit(solution)/shard_map/psum | solution.py:73
  122.5 0.0 all-gather.4.cloned.1.call-update
  122.6 0.6 gather_fusion.2
  123.3 0.1 copy.33
  123.3 0.7 gather_fusion.3
  124.0 0.1 copy.34
  124.1 0.1 mul.71
  124.2 2.8 %fusion.4 = bf16[1024,128]{0,1:T(8,128)(2,1)} fusion(bf16[1024,1024]{1,0:T(8,128)(2,1)} %param.15, bf16[128,1024]{1,0:T(8,128)(2,1)S(1)} %gather_fusion.1, pred[128]{0:T(512)(128)(4,1)S(1)} %compare_and_fusion.1), kind=kOutput, calls=%fused_computation.14 | convolution fusion | flops 268697600 | bytes 2621568 | tf_op jit(solution)/shard_map/td,de->et/dot_general | solution.py:30
  127.0 1.1 copy.35
  128.1 3.8 %while.29 = (s32[]{:T(128)}, f32[16,64,64]{2,1,0:T(8,128)S(1)}, s32[]{:T(128)}, f32[4,16,64,64]{3,2,1,0:T(8,128)}, s32[]{:T(128)}, /*index=5*/s32[]{:T(128)}) while((s32[]{:T(128)}, f32[16,64,64]{2,1,0:T(8,128)S(1)}, s32[]{:T(128)}, f32[4,16,64,64]{3,2,1,0:T(8,128)}, s32[]{:T(128)}, /*index=5*/s32[]{:T(128)}) %tuple.74), condition=%wide.region_9.10_spmd.clone, body=%wide.region_8.9_spmd.clone.sunk | while | flops 196612 | bytes 786525 | solution.py:20
  128.1 1.2 add_select_fusion.6
  129.4 1.2 add_select_fusion.6
  130.6 1.3 add_select_fusion.6
  131.9 27.5 %all-gather.4.cloned.1.call-done = f32[4,16,64,64]{3,2,1,0:T(8,128)} async-done(((f32[1,16,64,64]{3,2,1,0:T(8,128)}), f32[4,16,64,64]{3,2,1,0:T(8,128)}) %all-gather.4.cloned.1.call-update) | async-done | bytes 1048592 | tf_op jit(solution)/shard_map/all_gather | solution.py:13
  159.4 3.7 %while.28 = (s32[]{:T(128)}, f32[16,64,64]{2,1,0:T(8,128)S(1)}, s32[]{:T(128)}, f32[4,16,64,64]{3,2,1,0:T(8,128)}, s32[]{:T(128)}, /*index=5*/s32[]{:T(128)}) while((s32[]{:T(128)}, f32[16,64,64]{2,1,0:T(8,128)S(1)}, s32[]{:T(128)}, f32[4,16,64,64]{3,2,1,0:T(8,128)}, s32[]{:T(128)}, /*index=5*/s32[]{:T(128)}) %tuple.62), condition=%wide.region_7.8_spmd.clone, body=%wide.region_6.7_spmd.clone.sunk | while | flops 196612 | bytes 786525 | solution.py:20
  159.4 1.2 add_select_fusion.5
  160.6 1.2 add_select_fusion.5
  161.9 1.2 add_select_fusion.5
  163.1 1.4 fusion.6
  164.5 1.9 %multiply_reduce_fusion = (f32[16,128]{1,0:T(8,128)S(1)}, f32[16,64,128]{2,1,0:T(8,128)S(1)}) fusion(f32[16,64,128]{2,1,0:T(8,128)} %fusion.6, bf16[16,64,128]{2,1,0:T(8,128)(2,1)} %bitcast.74, bf16[16,64,128]{2,1,0:T(8,128)(2,1)S(1)} %bitcast.72, bf16[16,64,128]{2,1,0:T(8,128)(2,1)} %bitcast.76, pred[128,128]{1,0:T(8,128)(4,1)S(1)} %copy.34), kind=kOutput, calls=%fused_computation.17 | convolution fusion | flops 68024320 | bytes 1859584 | tf_op jit(solution)/shard_map/hts,hes->het/dot_general | solution.py:80
  166.4 0.2 multiply_convert_fusion
  166.6 2.9 %fusion.16 = f32[128,1024]{1,0:T(8,128)} fusion(bf16[1024,128]{1,0:T(8,128)(2,1)S(1)} %bitcast.78, bf16[1024,1024]{1,0:T(8,128)(2,1)} %param.19), kind=kOutput, calls=%fused_computation.61 | convolution fusion | flops 268435456 | bytes 2883584 | tf_op jit(solution)/shard_map/dt,de->te/dot_general | solution.py:88
  (25 shorter events, 0.1 us)
Async XLA Ops:
  6.5 26.4 %copy-start = (bf16[1024,1024]{1,0:T(8,128)(2,1)S(1)}, bf16[1024,1024]{1,0:T(8,128)(2,1)}, u32[]{:S(2)}) copy-start(bf16[1024,1024]{1,0:T(8,128)(2,1)} %param.17) | copy-start | bytes 6291460
  10.3 7.3 %copy-start.4 = (s32[1,4,4,2]{2,3,1,0:T(2,128)S(1)}, s32[1,4,4,2]{2,3,1,0:T(2,128)}, u32[]{:S(2)}) copy-start(s32[1,4,4,2]{2,3,1,0:T(2,128)} %param.13) | copy-start | bytes 388
  11.2 20.8 %all-to-all-start = ((bf16[4,64,1024]{2,1,0:T(8,128)(2,1)}), bf16[4,64,1024]{2,1,0:T(8,128)(2,1)S(1)}, u32[]{:S(2)}, u32[]{:S(2)}) async-start(bf16[4,64,1024]{2,1,0:T(8,128)(2,1)} %select_select_fusion), calls=%async_computation | async-start | bytes 1048576 | tf_op jit(solution)/shard_map/all_to_all | solution.py:63
  17.6 64.4 %all-gather.6.cloned.1.call-start = ((), (), s32[]{:S(2)}) async-start(), calls=%async_computation.3 | async-start | bytes 2621440 | tf_op jit(solution)/shard_map/all_gather | solution.py:13
  33.6 3.5 %copy-start.2 = (bf16[1024,128]{1,0:T(8,128)(2,1)}, bf16[1024,128]{1,0:T(8,128)(2,1)S(1)}, u32[]{:S(2)}) copy-start(bf16[1024,128]{1,0:T(8,128)(2,1)S(1)} %copy.32) | copy-start | bytes 786436
  35.8 86.8 %copy-start.1 = (s32[1,64,64]{2,1,0:T(8,128)S(1)}, s32[1,64,64]{2,1,0:T(8,128)}, u32[]{:S(2)}) copy-start(s32[1,64,64]{2,1,0:T(8,128)} %param.14) | copy-start | bytes 49156
  36.0 86.5 %copy-start.3 = (bf16[1024,128]{1,0:T(8,128)(2,1)}, bf16[1024,128]{1,0:T(8,128)(2,1)S(1)}, u32[]{:S(2)}) copy-start(bf16[1024,128]{1,0:T(8,128)(2,1)S(1)} %copy.36) | copy-start | bytes 786436
  36.0 88.1 %copy-start.5 = (f32[1024]{0:T(1024)S(1)}, f32[1024]{0:T(1024)}, u32[]{:S(2)}) copy-start(f32[1024]{0:T(1024)} %param.18) | copy-start | bytes 12292
  82.0 40.5 %all-reduce.2.cloned.1.call-start = ((), (), s32[]{:S(2)}) async-start(), calls=%async_computation.1 | async-start | bytes 1048576 | tf_op jit(solution)/shard_map/psum | solution.py:73
  82.8 76.6 %all-gather.4.cloned.1.call-start = ((), (), s32[]{:S(2)}) async-start(), calls=%async_computation.2 | async-start | bytes 2621440 | tf_op jit(solution)/shard_map/all_gather | solution.py:13
Sparse Core Ops, SparseCore 0:
  37.2 44.7 all-gather.5
  85.2 37.3 all-reduce.1
  124.4 34.9 all-gather.3
where the time goes:
time: 177 us; the launch traced here: 176 us
  waiting for transfers between devices  127 us (72%)
  between operations  13.3 us (8%)
  matrix products  12.7 us (7%)
  other arithmetic  10.2 us (6%)
  local copies, waits for them, and re-layouts  6.54 us (4%)
  starting transfers between devices  6.39 us (4%)
    all_gather x2, waiting for transfers between devices, prefix_2(): pieces = lax.all_gather(value, axis)  72.4 us
    psum x1, waiting for transfers between devices, body(): group_sum = lax.psum(state, 'seqi')  39.7 us
    all_to_all x1, waiting for transfers between devices, body(): lax.all_to_all(slots, 'seqi', split_axis=0, concat_axis=0, tiled=True)  14 us
    select_n x6, other arithmetic, turn(): return jnp.where(position < mine, longer, so_far)  7.41 us
    all_to_all x1, starting transfers between devices, body(): lax.all_to_all(slots, 'seqi', split_axis=0, concat_axis=0, tiled=True)  6.35 us
    dot_general x3, matrix products, project_columns(): jnp.einsum('td,de->et', rows, weight, preferred_element_type=jnp.float32)  5.45 us
  transfers between devices with their start and end apart: 4, of which 4 were waited for; matrix products, arithmetic and copies ran while one was open for 6% of the time, Pallas kernels for 0%

commit v1 on v0

--- a/solution.py
+++ b/solution.py
@@ -70,7 +70,8 @@
     state = jnp.einsum("hdt,het->hde", key_heads, value_heads, preferred_element_type=jnp.float32)
     zero_state = jnp.zeros_like(state)
     inner = prefix_2(state, "seqi", add_states, zero_state)
-    group_sum = lax.psum(state, "seqi")
+    parts = lax.all_gather(state, "seqi")
+    group_sum = jnp.sum(parts, axis=0)
     outer = prefix_2(group_sum, "seqo", add_states, zero_state)
     prefix = outer + inner
     scores = jnp.einsum("hdt,hds->hts", query_heads, key_heads, preferred_element_type=jnp.float32)

time: 177 us -> 136 us (0.77)
  waiting for transfers between devices: 127 us -> 83.5 us
  other arithmetic: 10.2 us -> 12.9 us
    all_gather x2 -> x1, waiting for transfers between devices: 72.4 us -> 24.6 us  [prefix_2(): pieces = lax.all_gather(value, axis)]
    all_gather x0 -> x1, waiting for transfers between devices: none -> 44.9 us  [body(): parts = lax.all_gather(state, 'seqi')]
    psum x1 -> x0, waiting for transfers between devices: 39.7 us -> none  [body(): group_sum = lax.psum(state, 'seqi')]
    reduce_sum x0 -> x1, other arithmetic: none -> 2.66 us  [body(): group_sum = jnp.sum(parts, axis=0)]
  transfers between devices with their start and end apart: 4 -> 3, of which waited for: 4 -> 3; matrix products, arithmetic and copies ran while one was open for 6% -> 7% of each run, Pallas kernels for 0% -> 0%
where the time goes in v1:
time: 136 us
  waiting for transfers between devices  83.5 us (61%)
  between operations  13.6 us (10%)
  other arithmetic  12.9 us (9%)
  matrix products  12.7 us (9%)
  local copies, waits for them, and re-layouts  6.55 us (5%)
  starting transfers between devices  6.39 us (5%)
    all_gather x1, waiting for transfers between devices, body(): parts = lax.all_gather(state, 'seqi')  44.9 us
    all_gather x1, waiting for transfers between devices, prefix_2(): pieces = lax.all_gather(value, axis)  24.6 us
    all_to_all x1, waiting for transfers between devices, body(): lax.all_to_all(slots, 'seqi', split_axis=0, concat_axis=0, tiled=True)  14 us
    select_n x6, other arithmetic, turn(): return jnp.where(position < mine, longer, so_far)  7.51 us
    all_to_all x1, starting transfers between devices, body(): lax.all_to_all(slots, 'seqi', split_axis=0, concat_axis=0, tiled=True)  6.35 us
    dot_general x3, matrix products, project_columns(): jnp.einsum('td,de->et', rows, weight, preferred_element_type=jnp.float32)  5.46 us
    dot_general x1, matrix products, body(): jnp.einsum('dt,de->te', normed, w_out, preferred_element_type=jnp.float32)  2.86 us
  transfers between devices with their start and end apart: 3, of which 3 were waited for; matrix products, arithmetic and copies ran while one was open for 7% of the time, Pallas kernels for 0%

profile of v1, /device:TPU:0, one launch (start us, length us, event | category | flops | bytes accessed | tf_op | source)
XLA Modules:
  0.0 135.8 jit_solution(4298760954927290589)
XLA Ops:
  6.5 0.0 copy-start
  6.5 0.9 multiply_reduce_fusion.1
  7.5 0.1 iota_compare_fusion
  7.5 0.1 add_select_fusion.2
  7.6 0.1 select_n.137
  7.7 2.5 %gather_fusion = bf16[256,1024]{1,0:T(8,128)(2,1)S(1)} fusion(bf16[128,1024]{1,0:T(8,128)(2,1)} %param.12, s32[1024]{0:T(1024)S(1)} %pad_clamp_fusion.2), kind=kCustom, calls=%fused_computation | custom fusion | bytes 1049600 | tf_op jit(solution)/shard_map/jit(_take)/gather | solution.py:51
  10.3 0.0 copy-start.4
  10.3 0.9 select_select_fusion
  11.2 6.3 %all-to-all-start = ((bf16[4,64,1024]{2,1,0:T(8,128)(2,1)}), bf16[4,64,1024]{2,1,0:T(8,128)(2,1)S(1)}, u32[]{:S(2)}, u32[]{:S(2)}) async-start(bf16[4,64,1024]{2,1,0:T(8,128)(2,1)} %select_select_fusion), calls=%async_computation | async-start | bytes 1048576 | tf_op jit(solution)/shard_map/all_to_all | solution.py:63
  17.6 0.0 all-gather.5.cloned.1.call-start
  17.6 0.0 copy-done.4
  17.6 0.1 fusion.11
  17.7 0.2 reduce-window.7
  17.9 0.1 convert_reduce_fusion
  18.0 0.1 select_reduce_fusion
  18.1 14.0 %all-to-all-done = bf16[4,64,1024]{2,1,0:T(8,128)(2,1)S(1)} async-done(((bf16[4,64,1024]{2,1,0:T(8,128)(2,1)}), bf16[4,64,1024]{2,1,0:T(8,128)(2,1)S(1)}, u32[]{:S(2)}, u32[]{:S(2)}) %all-to-all-start) | async-done | bytes 524320 | tf_op jit(solution)/shard_map/all_to_all | solution.py:63
  32.1 0.9 gather_fusion.1
  32.9 0.0 copy-done
  32.9 0.5 fusion.3
  33.4 0.2 copy.32
  33.6 2.2 %fusion.5 = bf16[1024,128]{0,1:T(8,128)(2,1)S(1)} fusion(bf16[1024,1024]{1,0:T(8,128)(2,1)} %param.16, bf16[128,1024]{1,0:T(8,128)(2,1)S(1)} %gather_fusion.1, pred[128]{0:T(512)(128)(4,1)S(1)} %compare_and_fusion.1), kind=kOutput, calls=%fused_computation.15 | convolution fusion | flops 268697600 | bytes 2621568 | tf_op jit(solution)/shard_map/td,de->et/dot_general | solution.py:30
  35.8 0.2 copy.36
  36.0 1.1 fusion.15
  37.0 0.0 all-gather.5.cloned.1.call-update
  37.1 0.0 all-gather.7.cloned.1.call-start
  37.1 44.9 %all-gather.5.cloned.1.call-done = f32[64,64,64]{2,1,0:T(8,128)} async-done(((f32[16,64,64]{2,1,0:T(8,128)}), f32[64,64,64]{2,1,0:T(8,128)}) %all-gather.5.cloned.1.call-update) | async-done | bytes 1048592 | tf_op jit(solution)/shard_map/all_gather | solution.py:73
  82.0 2.7 %reduce_sum.61 = f32[16,64,64]{2,1,0:T(8,128)} reduce(f32[4,16,64,64]{3,2,1,0:T(8,128)} %bitcast.68, f32[]{:T(128)} %constant.111.clone.1), dimensions={0}, to_apply=%region_5.6 | reduce | flops 196608 | bytes 1310724 | tf_op jit(solution)/shard_map/reduce_sum | solution.py:74
  84.7 0.0 all-gather.7.cloned.1.call-update
  84.7 0.6 gather_fusion.2
  85.4 0.1 copy.33
  85.5 0.7 gather_fusion.3
  86.1 0.1 copy.34
  86.3 0.1 mul.71
  86.3 2.8 %fusion.4 = bf16[1024,128]{0,1:T(8,128)(2,1)} fusion(bf16[1024,1024]{1,0:T(8,128)(2,1)} %param.15, bf16[128,1024]{1,0:T(8,128)(2,1)S(1)} %gather_fusion.1, pred[128]{0:T(512)(128)(4,1)S(1)} %compare_and_fusion.1), kind=kOutput, calls=%fused_computation.14 | convolution fusion | flops 268697600 | bytes 2621568 | tf_op jit(solution)/shard_map/td,de->et/dot_general | solution.py:30
  89.1 1.1 copy.35
  90.3 3.9 %while.29 = (s32[]{:T(128)}, f32[16,64,64]{2,1,0:T(8,128)S(1)}, s32[]{:T(128)}, f32[4,16,64,64]{3,2,1,0:T(8,128)}, s32[]{:T(128)}, /*index=5*/s32[]{:T(128)}) while((s32[]{:T(128)}, f32[16,64,64]{2,1,0:T(8,128)S(1)}, s32[]{:T(128)}, f32[4,16,64,64]{3,2,1,0:T(8,128)}, s32[]{:T(128)}, /*index=5*/s32[]{:T(128)}) %tuple.72), condition=%wide.region_9.10_spmd.clone, body=%wide.region_8.9_spmd.clone.sunk | while | flops 196612 | bytes 786525 | solution.py:20
  90.3 1.3 add_select_fusion.6
  91.6 1.3 add_select_fusion.6
  92.9 1.2 add_select_fusion.6
  94.2 24.6 %all-gather.7.cloned.1.call-done = f32[64,64,64]{2,1,0:T(8,128)} async-done(((f32[16,64,64]{2,1,0:T(8,128)}), f32[64,64,64]{2,1,0:T(8,128)}) %all-gather.7.cloned.1.call-update) | async-done | bytes 1048592 | tf_op jit(solution)/shard_map/all_gather | solution.py:13
  118.8 3.7 %while.28 = (s32[]{:T(128)}, f32[16,64,64]{2,1,0:T(8,128)S(1)}, s32[]{:T(128)}, f32[4,16,64,64]{3,2,1,0:T(8,128)}, s32[]{:T(128)}, /*index=5*/s32[]{:T(128)}) while((s32[]{:T(128)}, f32[16,64,64]{2,1,0:T(8,128)S(1)}, s32[]{:T(128)}, f32[4,16,64,64]{3,2,1,0:T(8,128)}, s32[]{:T(128)}, /*index=5*/s32[]{:T(128)}) %tuple.73), condition=%wide.region_7.8_spmd.clone, body=%wide.region_6.7_spmd.clone.sunk | while | flops 196612 | bytes 786525 | solution.py:20
  118.8 1.2 add_select_fusion.5
  120.1 1.2 add_select_fusion.5
  121.3 1.2 add_select_fusion.5
  122.6 1.4 %fusion.6 = f32[16,64,128]{2,1,0:T(8,128)} fusion(bf16[16,64,128]{2,1,0:T(8,128)(2,1)S(1)} %bitcast.72, f32[16,64,64]{2,1,0:T(8,128)S(1)} %get-tuple-element.163, f32[16,64,64]{2,1,0:T(8,128)S(1)} %get-tuple-element.164), kind=kOutput, calls=%fused_computation.18 | convolution fusion | flops 100728832 | bytes 1310720 | tf_op jit(solution)/shard_map/hdt,hde->het/dot_general | solution.py:82
  124.0 1.9 %multiply_reduce_fusion = (f32[16,128]{1,0:T(8,128)S(1)}, f32[16,64,128]{2,1,0:T(8,128)S(1)}) fusion(f32[16,64,128]{2,1,0:T(8,128)} %fusion.6, bf16[16,64,128]{2,1,0:T(8,128)(2,1)} %bitcast.75, bf16[16,64,128]{2,1,0:T(8,128)(2,1)S(1)} %bitcast.73, bf16[16,64,128]{2,1,0:T(8,128)(2,1)} %bitcast.77, pred[128,128]{1,0:T(8,128)(4,1)S(1)} %copy.34), kind=kOutput, calls=%fused_computation.17 | convolution fusion | flops 68024320 | bytes 1859584 | tf_op jit(solution)/shard_map/hts,hes->het/dot_general | solution.py:81
  125.9 0.2 multiply_convert_fusion
  126.1 2.9 %fusion.16 = f32[128,1024]{1,0:T(8,128)} fusion(bf16[1024,128]{1,0:T(8,128)(2,1)S(1)} %bitcast.79, bf16[1024,1024]{1,0:T(8,128)(2,1)} %param.19), kind=kOutput, calls=%fused_computation.61 | convolution fusion | flops 268435456 | bytes 2883584 | tf_op jit(solution)/shard_map/dt,de->te/dot_general | solution.py:89
  (23 shorter events, 0.1 us)
Async XLA Ops:
  6.5 26.4 %copy-start = (bf16[1024,1024]{1,0:T(8,128)(2,1)S(1)}, bf16[1024,1024]{1,0:T(8,128)(2,1)}, u32[]{:S(2)}) copy-start(bf16[1024,1024]{1,0:T(8,128)(2,1)} %param.17) | copy-start | bytes 6291460
  10.3 7.3 %copy-start.4 = (s32[1,4,4,2]{2,3,1,0:T(2,128)S(1)}, s32[1,4,4,2]{2,3,1,0:T(2,128)}, u32[]{:S(2)}) copy-start(s32[1,4,4,2]{2,3,1,0:T(2,128)} %param.13) | copy-start | bytes 388
  11.2 20.8 %all-to-all-start = ((bf16[4,64,1024]{2,1,0:T(8,128)(2,1)}), bf16[4,64,1024]{2,1,0:T(8,128)(2,1)S(1)}, u32[]{:S(2)}, u32[]{:S(2)}) async-start(bf16[4,64,1024]{2,1,0:T(8,128)(2,1)} %select_select_fusion), calls=%async_computation | async-start | bytes 1048576 | tf_op jit(solution)/shard_map/all_to_all | solution.py:63
  17.6 64.4 %all-gather.5.cloned.1.call-start = ((), (), s32[]{:S(2)}) async-start(), calls=%async_computation.1 | async-start | bytes 2621440 | tf_op jit(solution)/shard_map/all_gather | solution.py:73
  33.6 3.4 %copy-start.2 = (bf16[1024,128]{1,0:T(8,128)(2,1)}, bf16[1024,128]{1,0:T(8,128)(2,1)S(1)}, u32[]{:S(2)}) copy-start(bf16[1024,128]{1,0:T(8,128)(2,1)S(1)} %copy.32) | copy-start | bytes 786436
  36.0 48.7 %copy-start.3 = (bf16[1024,128]{1,0:T(8,128)(2,1)}, bf16[1024,128]{1,0:T(8,128)(2,1)S(1)}, u32[]{:S(2)}) copy-start(bf16[1024,128]{1,0:T(8,128)(2,1)S(1)} %copy.36) | copy-start | bytes 786436
  37.0 47.7 %copy-start.1 = (s32[1,64,64]{2,1,0:T(8,128)S(1)}, s32[1,64,64]{2,1,0:T(8,128)}, u32[]{:S(2)}) copy-start(s32[1,64,64]{2,1,0:T(8,128)} %param.14) | copy-start | bytes 49156
  37.1 81.8 %all-gather.7.cloned.1.call-start = ((), (), s32[]{:S(2)}) async-start(), calls=%async_computation.2 | async-start | bytes 2621440 | tf_op jit(solution)/shard_map/all_gather | solution.py:13
  82.0 4.3 %copy-start.5 = (f32[1024]{0:T(1024)S(1)}, f32[1024]{0:T(1024)}, u32[]{:S(2)}) copy-start(f32[1024]{0:T(1024)} %param.18) | copy-start | bytes 12292
Sparse Core Ops, SparseCore 0:
  37.2 44.7 all-gather.4
  84.8 33.9 all-gather.6
